TPU v7x, 256 devices: a whole 4x4x8 slice. The times are simulated.
256 devices in a mesh: layer: 16 (over z_hi, y, core), phi: 16 (over x, z_lo).
Axes of the slice: x: 4, y: 4, z: 8 (z_hi: 2, z_lo: 4; z = z_hi * 4 + z_lo), core: 2. Of those that a mesh axis runs over, the one named last changes fastest.
Arguments:
- features: bfloat16 [65536, 256], P(('layer', 'phi')), may hold values from -6 to 6
- w_layers: bfloat16 [4, 256, 256], replicated, may hold values from -0.375 to 0.375
- b_layers: float32 [4, 256], replicated, may hold values from -1.5 to 1.5
- w_coord: bfloat16 [16, 256], replicated, may hold values from -0.09375 to 0.09375
- w_beta: bfloat16 [256], replicated, may hold values from -0.375 to 0.375
- point_hit: int32 [2048], P(('layer', 'phi')), may hold values from 0 to 255
- track: int32 [65536], P(('layer', 'phi')), may hold values from 0 to 2047
- noise: int32 [65536], P(('layer', 'phi')), may hold values 0 or 1
Outputs:
- grad_w_layers: float32 [4, 256, 256], replicated
- grad_b_layers: float32 [4, 256], replicated
- grad_w_coord: float32 [16, 256], replicated
- grad_w_beta: float32 [256], replicated
- loss: float32 [], replicated
Inputs may be any that keep to these rules, and one draw needn't show every extreme that they name: `point_hit`: an index among the 256 hits of the device holding the entry. A non-noise hit of track k is attracted to point k.
All inputs are finite; a program needn't handle non-finite values. No bound on the sum of `noise` on one device may be relied on, other than what follows from the above.
Results may differ from a plain program's by a relative error of at most 0.0013.
Values sent between devices are 32-bit elements; how exact they have to be, the bound alone decides.
A program may use at most 64 MiB of HBM per device.

v0:
```python
import jax
import jax.numpy as jnp
from jax import lax
from jax.sharding import PartitionSpec as P

dist_eps = 0.0001
charge_floor = 0.5
block_cols = 512


def mlp_forward(features, w_layers, b_layers, w_coord, w_beta):
    hidden = features
    states = [features]
    preacts = []
    for layer_num in range(w_layers.shape[0]):
        pre = (
            jnp.dot(hidden, w_layers[layer_num], preferred_element_type=jnp.float32)
            + b_layers[layer_num]
        )
        preacts.append(pre)
        hidden = jax.nn.silu(pre).astype(jnp.bfloat16)
        states.append(hidden)
    coords = lax.dot_general(
        w_coord, hidden, (((1,), (1,)), ((), ())), preferred_element_type=jnp.float32
    )
    logits = jnp.dot(hidden, w_beta, preferred_element_type=jnp.float32)
    return (states, preacts, coords, logits)


def charges(logits):
    expz = jnp.exp(logits)
    spread = jnp.log1p(2.0 * expz)
    charge = 0.25 * spread * spread + charge_floor
    slope = 0.5 * spread * (2.0 * expz / (1.0 + 2.0 * expz))
    return (jax.nn.sigmoid(logits), charge, slope)


def pair_terms(coords, charge, track, live, point_rows, first, hits_all):
    point_y = point_rows[:-1]
    point_q = point_rows[-1]
    width = point_rows.shape[1]
    hit_sq = jnp.sum(coords * coords, 0)
    point_sq = jnp.sum(point_y * point_y, 0)
    cross = lax.dot_general(
        coords,
        point_y,
        (((0,), (0,)), ((), ())),
        precision=lax.Precision.HIGHEST,
        preferred_element_type=jnp.float32,
    )
    dist_sq = jnp.maximum(hit_sq[:, None] + point_sq[None, :] - 2.0 * cross, 0.0)
    dist = jnp.sqrt(dist_sq + dist_eps)
    index = first + lax.iota(jnp.int32, width)
    match = jnp.where((track[:, None] == index[None, :]) & (live[:, None] > 0), 1.0, 0.0)
    reach = jnp.maximum(1.0 - dist, 0.0)
    potential = match * dist_sq + (1.0 - match) * reach * reach
    pot_rows = jnp.sum(potential * point_q[None, :], 1)
    coef = (
        (charge / hits_all)[:, None]
        * point_q[None, :]
        * (2.0 * match - (1.0 - match) * 2.0 * reach / dist)
    )
    row_sums = jnp.sum(coef, 1)
    col_sums = jnp.sum(coef, 0)
    pulls = lax.dot_general(
        point_y,
        coef,
        (((1,), (1,)), ((), ())),
        precision=lax.Precision.HIGHEST,
        preferred_element_type=jnp.float32,
    )
    point_grad = point_y * col_sums[None, :] - lax.dot_general(
        coords,
        coef,
        (((1,), (0,)), ((), ())),
        precision=lax.Precision.HIGHEST,
        preferred_element_type=jnp.float32,
    )
    charge_grad = jnp.dot(charge, potential, precision=lax.Precision.HIGHEST) / hits_all
    return (row_sums, pot_rows, pulls, jnp.concatenate([point_grad, charge_grad[None, :]], 0))


def on_device(features, w_layers, b_layers, w_coord, w_beta, point_hit, track, noise):
    hit_count = features.shape[0]
    point_count = point_hit.shape[0]
    ndev = lax.axis_size("layer") * lax.axis_size("phi")
    total_points = point_count * ndev
    hits_all = hit_count * ndev * 1.0
    states, preacts, coords, logits = mlp_forward(features, w_layers, b_layers, w_coord, w_beta)
    beta_vals, charge, slope = charges(logits)
    selector = jnp.where(point_hit[:, None] == lax.iota(jnp.int32, hit_count)[None, :], 1.0, 0.0)
    own_y = lax.dot_general(
        coords,
        selector,
        (((1,), (1,)), ((), ())),
        precision=lax.Precision.HIGHEST,
        preferred_element_type=jnp.float32,
    )
    own_q = jnp.dot(selector, charge, precision=lax.Precision.HIGHEST)
    own_beta = jnp.dot(selector, beta_vals, precision=lax.Precision.HIGHEST)
    own_rows = jnp.concatenate([own_y, own_q[None, :]], 0)
    live = 1 - noise
    init = (
        jnp.zeros((hit_count,), jnp.float32),
        jnp.zeros((hit_count,), jnp.float32),
        jnp.zeros(coords.shape, jnp.float32),
        jnp.zeros((own_rows.shape[0], total_points), jnp.float32),
    )
    piece = lax.all_gather(own_rows, ("layer", "phi"), axis=1, tiled=True)
    width = piece.shape[1]

    def one_block(state, offset, cols):
        row_acc, pot_acc, pull_acc, grad_acc = state
        block = lax.dynamic_slice_in_dim(piece, offset, cols, 1)
        row_sums, pot_rows, pulls, point_grads = pair_terms(
            coords, charge, track, live, block, offset, hits_all
        )
        grad_acc = lax.dynamic_update_slice_in_dim(grad_acc, point_grads, offset, 1)
        return (row_acc + row_sums, pot_acc + pot_rows, pull_acc + pulls, grad_acc)

    full = width // block_cols
    state = init
    state = lax.fori_loop(
        0, full, lambda step, inner: one_block(inner, step * block_cols, block_cols), state
    )
    row_sums, pot_rows, pulls, point_grads = state
    own_grads = lax.psum_scatter(point_grads, ("layer", "phi"), scatter_dimension=1, tiled=True)
    coord_dim = coords.shape[0]
    coord_grad = coords * row_sums[None, :] - pulls
    coord_grad = coord_grad + jnp.dot(
        own_grads[:coord_dim], selector, precision=lax.Precision.HIGHEST
    )
    charge_grad = pot_rows / hits_all + jnp.dot(
        own_grads[coord_dim], selector, precision=lax.Precision.HIGHEST
    )
    noise_float = noise.astype(jnp.float32)
    beta_grad = noise_float / hits_all + jnp.sum(selector, 0) * (-1.0 / total_points)
    logit_grad = charge_grad * slope + beta_grad * beta_vals * (1.0 - beta_vals)
    loss_local = (
        jnp.sum(charge * pot_rows) / hits_all
        + jnp.sum(1.0 - own_beta) / total_points
        + jnp.sum(noise_float * beta_vals) / hits_all
    )
    coord_low = coord_grad.astype(jnp.bfloat16)
    logit_low = logit_grad.astype(jnp.bfloat16)
    hidden = states[-1]
    grad_coord_w = lax.dot_general(
        coord_low, hidden, (((1,), (0,)), ((), ())), preferred_element_type=jnp.float32
    )
    grad_beta_w = jnp.dot(logit_low, hidden, preferred_element_type=jnp.float32)
    upstream = lax.dot_general(
        coord_low, w_coord, (((0,), (0,)), ((), ())), preferred_element_type=jnp.float32
    )
    upstream = (
        upstream + logit_low.astype(jnp.float32)[:, None] * w_beta.astype(jnp.float32)[None, :]
    )
    count = w_layers.shape[0]
    weight_grads = [None] * count
    bias_grads = [None] * count
    for layer_num in range(count - 1, -1, -1):
        pre = preacts[layer_num]
        sig = jax.nn.sigmoid(pre)
        local = (upstream * sig * (1.0 + pre * (1.0 - sig))).astype(jnp.bfloat16)
        weight_grad = lax.dot_general(
            states[layer_num], local, (((0,), (0,)), ((), ())), preferred_element_type=jnp.float32
        )
        bias_grad = jnp.sum(local.astype(jnp.float32), 0)
        if layer_num > 0:
            upstream = lax.dot_general(
                local,
                w_layers[layer_num],
                (((1,), (1,)), ((), ())),
                preferred_element_type=jnp.float32,
            )
        weight_grads[layer_num] = weight_grad
        bias_grads[layer_num] = bias_grad
    grad_w_layers = jnp.stack(weight_grads)
    grad_b_layers = jnp.stack(bias_grads)
    grad_w_layers, grad_b_layers, grad_coord_w, grad_beta_w, loss_local = lax.psum(
        (grad_w_layers, grad_b_layers, grad_coord_w, grad_beta_w, loss_local), ("layer", "phi")
    )
    return (grad_w_layers, grad_b_layers, grad_coord_w, grad_beta_w, loss_local)


def solution(mesh):
    return jax.shard_map(
        on_device,
        mesh=mesh,
        in_specs=(
            P(("layer", "phi"), None),
            P(),
            P(),
            P(),
            P(),
            P(("layer", "phi")),
            P(("layer", "phi")),
            P(("layer", "phi")),
        ),
        out_specs=(P(), P(), P(), P(), P()),
        check_vma=False,
    )
```

profile of v0, /device:TPU:2, one launch (start us, length us, event | category | flops | bytes accessed | tf_op | source)
XLA Modules:
  0.0 1170.9 jit_solution(12711560222220822224)
XLA Ops:
  7.3 0.7 reshape.37
  8.0 0.7 broadcast_subtract_fusion
  8.7 0.8 fusion.82
  9.5 1.1 convolution_add_fusion.4
  11.5 0.7 copy-done.3
  13.0 0.6 copy-done.7
  14.1 626.3 %all_gather.3 = f32[17,2048]{0,1:T(8,128)S(1)} all-gather(f32[17,8]{0,1:T(8,128)S(1)} %pad_maximum_fusion.1), channel_id=1, replica_groups=mesh['layer'=16,'phi'=16] {'layer','phi'}, dimensions={1}, use_global_device_ids=true | all-gather | bytes 139808 | tf_op jit(solution)/shard_map/all_gather | solution.py:109
  640.8 0.7 copy-done.5
  641.5 11.6 while.22
  641.6 1.3 multiply_reduce_fusion.8
  644.5 1.3 multiply_reduce_fusion.8
  647.4 1.3 multiply_reduce_fusion.8
  650.3 1.3 multiply_reduce_fusion.8
  653.1 0.7 copy-done.1
  653.9 0.6 copy-done.6
  654.5 0.8 fusion.25
  656.7 243.4 %all-reduce.7.cloned.1.call-done = f32[17,2048]{1,0:T(8,128)} async-done(((f32[17,2048]{1,0:T(8,128)}), f32[17,2048]{1,0:T(8,128)}) %all-reduce.7.cloned.1.call-update) | async-done | bytes 139280
  900.1 0.9 fusion.41
  901.0 0.6 fusion.81
  901.6 0.9 fusion.23
  905.2 1.0 pad_maximum_fusion
  906.6 75.0 %all-reduce.1 = (f32[4,256]{1,0:T(4,128)}, f32[16,256]{1,0:T(8,128)}, f32[256]{0:T(256)}, f32[]{:T(128)}) all-reduce(f32[4,256]{1,0:T(4,128)S(1)} %pad_maximum_fusion.2, f32[16,256]{1,0:T(8,128)S(1)} %fusion.85, f32[256]{0:T(256)S(1)} %bitcast.138, f32[]{:T(128)S(6)} %add.271), channel_id=1, replica_groups=mesh['layer'=16,'phi'=16] {'layer','phi'}, use_global_device_ids=true, to_apply=%region_14.15 | all-reduce | flops 5377 | bytes 43016 | tf_op jit(solution)/shard_map/psum | solution.py:179
  981.6 180.0 %all-reduce.5.cloned.1.call-done = f32[4,256,256]{1,2,0:T(8,128)} async-done(((f32[4,256,256]{1,2,0:T(8,128)}), f32[4,256,256]{1,2,0:T(8,128)}) %all-reduce.5.cloned.1.call-update) | async-done | bytes 1048592 | tf_op jit(solution)/shard_map/psum | solution.py:179
  1161.6 2.5 copy.30
  (87 shorter events, 11.0 us)
Async XLA Ops:
  7.2 2.4 copy-start
  7.2 3.4 copy-start.2
  7.2 892.9 %all-reduce.7.cloned.1.call-start = ((), (), s32[]{:S(2)}) async-start(), calls=%async_computation.1 | async-start | bytes 393216
  11.3 1.5 copy-start.4
  11.5 0.7 copy-start.3
  13.0 0.7 copy-start.7
  640.8 0.7 copy-start.5
  653.1 0.7 copy-start.1
  653.8 507.8 %all-reduce.5.cloned.1.call-start = ((), (), s32[]{:S(2)}) async-start(), calls=%async_computation | async-start | bytes 2097152 | tf_op jit(solution)/shard_map/psum | solution.py:179
  653.9 0.7 copy-start.6
Sparse Core Ops, SparseCore 0:
  653.9 246.1 all-reduce.6
  906.4 255.1 all-reduce.4
where the time goes:
time: 1170 us
  blocking collectives  701 us (60%)
  waiting for transfers between devices  423 us (36%)
  matrix products  18.3 us (2%)
  between operations  16.2 us (1%)
    all_gather x1, blocking collectives, on_device(): piece = lax.all_gather(own_rows, ('layer', 'phi'), axis=1, tiled=True)  626 us
    unnamed x3, waiting for transfers between devices  243 us
    psum x1, waiting for transfers between devices, on_device(): lax.psum((grad_w_layers, grad_b_layers, grad_coord_w, grad_beta_w, loss_l...  180 us
    psum x1, blocking collectives, on_device(): lax.psum((grad_w_layers, grad_b_layers, grad_coord_w, grad_beta_w, loss_l...  75 us
  transfers between devices with their start and end apart: 2, of which 2 were waited for; matrix products, arithmetic and copies ran while one was open for 0% of the time, Pallas kernels for 0%

commit v1 on v0

--- a/solution.py
+++ b/solution.py
@@ -106,7 +106,12 @@
         jnp.zeros(coords.shape, jnp.float32),
         jnp.zeros((own_rows.shape[0], total_points), jnp.float32),
     )
-    piece = lax.all_gather(own_rows, ("layer", "phi"), axis=1, tiled=True)
+    piece = jnp.concatenate(
+        lax.all_to_all(
+            jnp.stack([own_rows] * lax.axis_size(("layer", "phi"))), ("layer", "phi"), 0, 0
+        ),
+        axis=1,
+    )
     width = piece.shape[1]
 
     def one_block(state, offset, cols):

time: 1170 us -> 574 us (0.49)
  blocking collectives: 701 us -> 74.9 us
  starting transfers between devices: 0.08 us -> 14.8 us
    all_gather x1 -> x0, blocking collectives: 626 us -> none  [on_device(): piece = lax.all_gather(own_rows, ('layer', 'phi'), axis=1, tiled=True)]
    all_to_all x0 -> x1, starting transfers between devices: none -> 14.7 us  [on_device(): lax.all_to_all(jnp.stack([own_rows] * lax.axis_size(('layer', 'phi'))), (...]
    all_to_all x0 -> x1, waiting for transfers between devices: none -> 11.9 us  [on_device(): lax.all_to_all(jnp.stack([own_rows] * lax.axis_size(('layer', 'phi'))), (...]
  transfers between devices with their start and end apart: 2 -> 3, of which waited for: 2 -> 3; matrix products, arithmetic and copies ran while one was open for 0% -> 0% of each run, Pallas kernels for 0% -> 0%
where the time goes in v1:
time: 574 us; the launch traced here: 573 us
  waiting for transfers between devices  433 us (75%)
  blocking collectives  74.9 us (13%)
  matrix products  18.8 us (3%)
  between operations  16.2 us (3%)
  starting transfers between devices  14.8 us (3%)
  local copies, waits for them, and re-layouts  11.4 us (2%)
    unnamed x3, waiting for transfers between devices  241 us
    psum x1, waiting for transfers between devices, on_device(): lax.psum((grad_w_layers, grad_b_layers, grad_coord_w, grad_beta_w, loss_l...  180 us
    psum x1, blocking collectives, on_device(): lax.psum((grad_w_layers, grad_b_layers, grad_coord_w, grad_beta_w, loss_l...  74.9 us
    all_to_all x1, starting transfers between devices, on_device(): lax.all_to_all(jnp.stack([own_rows] * lax.axis_size(('layer', 'phi'))), (...  14.7 us
    all_to_all x1, waiting for transfers between devices, on_device(): lax.all_to_all(jnp.stack([own_rows] * lax.axis_size(('layer', 'phi'))), (...  11.9 us
  transfers between devices with their start and end apart: 3, of which 3 were waited for; matrix products, arithmetic and copies ran while one was open for 0% of the time, Pallas kernels for 0%

profile of v1, /device:TPU:2, one launch (start us, length us, event | category | flops | bytes accessed | tf_op | source)
XLA Modules:
  0.0 573.3 jit_solution(9517267390154085301)
XLA Ops:
  7.2 0.8 fusion.82
  8.1 1.1 convolution_add_fusion.4
  10.1 0.9 multiply_convert_fusion
  11.9 0.7 copy-done.3
  14.4 1.5 reshape.59
  16.0 14.7 %all-to-all-start = ((f32[256,1,136]{2,1,0:T(1,128)}), f32[256,1,136]{2,1,0:T(1,128)S(1)}, u32[]{:S(2)}, u32[]{:S(2)}) async-start(f32[256,1,136]{2,1,0:T(1,128)} %reshape.59), calls=%async_computation | async-start | bytes 524288 | tf_op jit(solution)/shard_map/all_to_all | solution.py:110
  30.7 0.8 fusion.25
  32.8 11.9 %all-to-all-done = f32[256,1,136]{2,1,0:T(1,128)S(1)} async-done(((f32[256,1,136]{2,1,0:T(1,128)}), f32[256,1,136]{2,1,0:T(1,128)S(1)}, u32[]{:S(2)}, u32[]{:S(2)}) %all-to-all-start) | async-done | bytes 139296 | tf_op jit(solution)/shard_map/all_to_all | solution.py:110
  45.3 1.3 reduce
  47.4 0.7 copy-done.5
  48.0 11.6 %while.22 = (s32[]{:T(128)}, f32[256]{0:T(256)S(1)}, f32[256]{0:T(256)S(1)}, f32[16,256]{1,0:T(8,128)S(1)}, f32[17,2048]{1,0:T(8,128)S(1)}, /*index=5*/f32[256]{...) while((s32[]{:T(128)}, f32[256]{0:T(256)S(1)}, ...), condition=%wide.region_6.7_spmd.clone, body=%wide.region_1.6_spmd.clone.sunk | while | flops 80528904 | bytes 2975734 | solution.py:128
  48.1 1.3 multiply_reduce_fusion.8
  51.0 1.3 multiply_reduce_fusion.8
  53.9 1.3 multiply_reduce_fusion.8
  56.8 1.3 multiply_reduce_fusion.8
  60.5 240.6 %all-reduce.7.cloned.1.call-done = f32[17,2048]{1,0:T(8,128)} async-done(((f32[17,2048]{1,0:T(8,128)}), f32[17,2048]{1,0:T(8,128)}) %all-reduce.7.cloned.1.call-update) | async-done | bytes 139280
  301.1 0.9 fusion.41
  302.6 0.9 fusion.23
  303.8 0.7 copy-done.9
  304.7 0.7 copy-done.11
  307.6 1.0 pad_maximum_fusion
  309.0 74.9 %all-reduce.1 = (f32[4,256]{1,0:T(4,128)}, f32[16,256]{1,0:T(8,128)}, f32[256]{0:T(256)}, f32[]{:T(128)}) all-reduce(f32[4,256]{1,0:T(4,128)S(1)} %pad_maximum_fusion.2, f32[16,256]{1,0:T(8,128)S(1)} %fusion.85, f32[256]{0:T(256)S(1)} %bitcast.146, f32[]{:T(128)S(6)} %add.271), channel_id=1, replica_groups=mesh['layer'=16,'phi'=16] {'layer','phi'}, use_global_device_ids=true, to_apply=%region_14.15 | all-reduce | flops 5377 | bytes 43016 | tf_op jit(solution)/shard_map/psum | solution.py:184
  383.9 180.1 %all-reduce.5.cloned.1.call-done = f32[4,256,256]{1,2,0:T(8,128)} async-done(((f32[4,256,256]{1,2,0:T(8,128)}), f32[4,256,256]{1,2,0:T(8,128)}) %all-reduce.5.cloned.1.call-update) | async-done | bytes 1048592 | tf_op jit(solution)/shard_map/psum | solution.py:184
  563.9 2.5 copy.36
  (104 shorter events, 14.8 us)
Async XLA Ops:
  7.2 0.9 copy-start
  7.2 0.9 copy-start.6
  7.2 2.0 copy-start.2
  9.4 0.7 copy-start.10
  10.1 0.9 copy-start.8
  11.0 0.7 copy-start.4
  11.9 0.7 copy-start.3
  13.2 0.7 copy-start.7
  16.0 28.8 %all-to-all-start = ((f32[256,1,136]{2,1,0:T(1,128)}), f32[256,1,136]{2,1,0:T(1,128)S(1)}, u32[]{:S(2)}, u32[]{:S(2)}) async-start(f32[256,1,136]{2,1,0:T(1,128)} %reshape.59), calls=%async_computation | async-start | bytes 524288 | tf_op jit(solution)/shard_map/all_to_all | solution.py:110
  30.6 270.5 %all-reduce.7.cloned.1.call-start = ((), (), s32[]{:S(2)}) async-start(), calls=%async_computation.2 | async-start | bytes 393216
  47.3 0.7 copy-start.5
  59.6 0.7 copy-start.1
  59.6 243.9 %copy-start.12 = (f32[256,256]{1,0:T(8,128)S(1)}, f32[256,256]{1,0:T(8,128)}, u32[]{:S(2)}) copy-start(f32[256,256]{1,0:T(8,128)} %get-tuple-element.386) | copy-start | bytes 786436
  60.3 503.6 %all-reduce.5.cloned.1.call-start = ((), (), s32[]{:S(2)}) async-start(), calls=%async_computation.1 | async-start | bytes 2097152 | tf_op jit(solution)/shard_map/psum | solution.py:184
  303.5 1.0 copy-start.9
  304.5 0.9 copy-start.11
Sparse Core Ops, SparseCore 0:
  60.4 240.6 all-reduce.6
  308.8 255.1 all-reduce.4
